TPU v7x, 32 devices: a whole 2x2x4 slice. The times are simulated.
32 devices in a mesh: seq: 8 (over z, core), head: 4 (over y, x).
Axes of the slice: x: 2, y: 2, z: 4, core: 2. Of those that a mesh axis runs over, the one named last changes fastest.
Arguments:
- video_query: bfloat16 [4096, 3072], P(('seq', 'head')), may hold values from -8 to 8
- video_key: bfloat16 [4096, 3072], P(('seq', 'head')), may hold values from -8 to 8
- video_value: bfloat16 [4096, 3072], P(('seq', 'head')), may hold values from -6 to 6
- video_grad: bfloat16 [4096, 3072], P(('seq', 'head')), may hold values from -6 to 6
- text_query: bfloat16 [256, 3072], P(None, 'head'), may hold values from -8 to 8
- text_key: bfloat16 [256, 3072], P(None, 'head'), may hold values from -8 to 8
- text_value: bfloat16 [256, 3072], P(None, 'head'), may hold values from -6 to 6
- text_grad: bfloat16 [256, 3072], P(None, 'head'), may hold values from -6 to 6
- tile_list: int32 [32, 8], replicated, may hold values from 0 to 31, as said below
- tile_count: int32 [32], replicated, may hold values from 1 to 8, as said below
- text_mask: int32 [256], replicated, may hold values from 0 to 1, as said below
Outputs:
- attended_video: bfloat16 [4096, 3072], P(('seq', 'head'))
- video_query_grad: bfloat16 [4096, 3072], P(('seq', 'head'))
- video_key_grad: bfloat16 [4096, 3072], P(('seq', 'head'))
- video_value_grad: bfloat16 [4096, 3072], P(('seq', 'head'))
- attended_text: bfloat16 [256, 3072], P(None, 'head')
- text_query_grad: bfloat16 [256, 3072], P(None, 'head')
- text_key_grad: bfloat16 [256, 3072], P(None, 'head')
- text_value_grad: bfloat16 [256, 3072], P(None, 'head')
Inputs may be any that keep to these rules, and one draw needn't show every extreme that they name: `tile_list`: the 8 entries of one query tile's list are distinct. Query tiles fall in aligned blocks of 4; the used entries of one block together name at most 2 distinct tiles of any other block of 4 tiles, and every block names exactly 2 from some other block. `tile_count`: every aligned block of 4 query tiles has a tile that uses all 8 entries. `text_mask`: the ones form a prefix of at least 64 entries.
All inputs are finite; a program needn't handle non-finite values.
Results may differ from a plain program's by a relative error of at most 0.012.
Values may be sent and summed in bfloat16 or wider, within the bound.
A program may use at most 192 MiB of HBM per device.

v0:
```python
import jax
import jax.numpy as jnp
from jax import lax
from jax.sharding import PartitionSpec as P

HD = 128
TXT = 256
TILE = 128
KT = 8
MOST = 2
NEGATIVE = -1e30
HIGHEST_PRECISION = lax.Precision.HIGHEST


def split_product(form, weights, data):
    upper = weights.astype(jnp.bfloat16)
    lower = (weights - upper.astype(jnp.float32)).astype(jnp.bfloat16)
    return jnp.einsum(form, upper, data, preferred_element_type=jnp.float32) + jnp.einsum(
        form, lower, data, preferred_element_type=jnp.float32
    )


def block_scores(query_blk, key_blk, live_blk, factor):
    scores = (
        jnp.einsum("bthd,bkhd->bhtk", query_blk, key_blk, preferred_element_type=jnp.float32)
        * factor
    )
    scores = jnp.where(live_blk[:, None, None, :], scores, NEGATIVE)
    maximum = jnp.max(scores, axis=-1)
    log_total = maximum + jnp.log(jnp.sum(jnp.exp(scores - maximum[..., None]), axis=-1))
    return (scores, log_total)


def block_forward(scores, log_total, value_blk, grad_blk):
    weights = jnp.exp(scores - log_total[..., None]).astype(jnp.bfloat16)
    output = jnp.einsum("bhtk,bkhd->bthd", weights, value_blk, preferred_element_type=jnp.float32)
    offset = jnp.sum(grad_blk.astype(jnp.float32) * output, axis=-1)
    return (output, jnp.transpose(offset, (0, 2, 1)))


def block_backward(scores, log_total, offset, query_blk, key_blk, value_blk, grad_blk, factor):
    probability = jnp.exp(scores - log_total[..., None])
    weights = probability.astype(jnp.bfloat16)
    prob_grad = jnp.einsum(
        "bthd,bkhd->bhtk", grad_blk, value_blk, preferred_element_type=jnp.float32
    )
    score_grad = (probability * (prob_grad - offset[..., None])).astype(jnp.bfloat16)
    query_grad = (
        jnp.einsum("bhtk,bkhd->bthd", score_grad, key_blk, preferred_element_type=jnp.float32)
        * factor
    )
    key_grad = (
        jnp.einsum("bhtk,bthd->bkhd", score_grad, query_blk, preferred_element_type=jnp.float32)
        * factor
    )
    value_grad = jnp.einsum(
        "bhtk,bthd->bkhd", weights, grad_blk, preferred_element_type=jnp.float32
    )
    return (query_grad, key_grad, value_grad)


def spread_grads(pool_total, text_total, grad_blk, pool_slot):
    block_tiles = grad_blk.shape[0]
    tile_part = grad_blk[:, : KT * TILE].reshape(block_tiles, KT, TILE, pool_total.shape[2])
    return (
        pool_total.at[pool_slot].add(tile_part),
        text_total + jnp.sum(grad_blk[:, KT * TILE :], axis=0),
    )


def body(
    video_query,
    video_key,
    video_value,
    video_grad,
    text_query,
    text_key,
    text_value,
    text_grad,
    tile_list,
    tile_count,
    text_mask,
):
    factor = HD ** (-0.5)
    groups = lax.axis_size("seq")
    own_group = lax.axis_index("seq")
    query_rows, key_rows, value_rows, grad_rows = (
        lax.all_to_all(video_query, "head", split_axis=1, concat_axis=0, tiled=True),
        lax.all_to_all(video_key, "head", split_axis=1, concat_axis=0, tiled=True),
        lax.all_to_all(video_value, "head", split_axis=1, concat_axis=0, tiled=True),
        lax.all_to_all(video_grad, "head", split_axis=1, concat_axis=0, tiled=True),
    )
    token_rows, feature_width = query_rows.shape
    head_count = feature_width // HD
    shard_tiles = token_rows // TILE
    tile_total = tile_list.shape[0]
    text_ok = text_mask > 0
    entry_live = jnp.arange(KT)[None, :] < tile_count[:, None]
    tile_hits = (tile_list[:, :, None] == jnp.arange(tile_total)[None, None, :]) & entry_live[
        :, :, None
    ]
    wanted = jnp.any(
        jnp.any(tile_hits, axis=1).reshape(groups, shard_tiles, tile_total), axis=1
    ).reshape(groups, groups, shard_tiles)
    slot_rank = jnp.cumsum(wanted.astype(jnp.int32), axis=2) - 1
    distinct = (jnp.arange(groups)[:, None] != jnp.arange(groups)[None, :])[:, :, None, None]
    select = (
        wanted[:, :, None, :]
        & (slot_rank[:, :, None, :] == jnp.arange(MOST)[None, None, :, None])
        & distinct
    )
    outgoing = lax.dynamic_index_in_dim(select, own_group, 1, keepdims=False)
    incoming = lax.dynamic_index_in_dim(select, own_group, 0, keepdims=False)
    picker = outgoing.reshape(groups * MOST, shard_tiles).astype(jnp.bfloat16)
    send_keys = jnp.dot(
        picker,
        key_rows.reshape(shard_tiles, TILE * feature_width),
        preferred_element_type=jnp.float32,
    )
    send_keys = send_keys.astype(jnp.bfloat16).reshape(groups, MOST * TILE, feature_width)
    send_values = jnp.dot(
        picker,
        value_rows.reshape(shard_tiles, TILE * feature_width),
        preferred_element_type=jnp.float32,
    )
    send_values = send_values.astype(jnp.bfloat16).reshape(groups, MOST * TILE, feature_width)
    owner_base = (
        jnp.arange(groups, dtype=jnp.int32)[:, None, None] * shard_tiles
        + jnp.arange(shard_tiles, dtype=jnp.int32)[None, None, :]
    )
    slot_ids = jnp.where(
        jnp.any(incoming, axis=2), jnp.sum(jnp.where(incoming, owner_base, 0), axis=2), -1
    ).reshape(groups * MOST)
    pool_ids = jnp.concatenate(
        [own_group * shard_tiles + jnp.arange(shard_tiles, dtype=jnp.int32), slot_ids]
    )
    pool_size = shard_tiles + groups * MOST
    my_list = lax.dynamic_slice_in_dim(tile_list, own_group * shard_tiles, shard_tiles, 0)
    my_count = lax.dynamic_slice_in_dim(tile_count, own_group * shard_tiles, shard_tiles, 0)
    pool_match = my_list[:, :, None] == pool_ids[None, None, :]
    pool_slot = jnp.sum(jnp.where(pool_match, jnp.arange(pool_size, dtype=jnp.int32), 0), axis=2)
    live_entry = jnp.any(pool_match, axis=2) & (jnp.arange(KT)[None, :] < my_count[:, None])
    text_query3 = text_query.reshape(TXT, head_count, HD)
    text_key3 = text_key.reshape(TXT, head_count, HD)
    text_value3 = text_value.reshape(TXT, head_count, HD)
    text_grad3 = text_grad.reshape(TXT, head_count, HD)
    block_tiles = min(shard_tiles, max(1, 512 // TILE))
    block_count = shard_tiles // block_tiles
    query_blocks = query_rows.reshape(block_count, block_tiles, TILE, head_count, HD)
    grad_blocks = grad_rows.reshape(block_count, block_tiles, TILE, head_count, HD)
    slot_blocks = pool_slot.reshape(block_count, block_tiles, KT)
    live_blocks = jnp.concatenate(
        [
            jnp.repeat(live_entry, TILE, axis=1),
            jnp.broadcast_to(text_ok[None, :], (shard_tiles, TXT)),
        ],
        axis=1,
    )
    live_blocks = live_blocks.reshape(block_count, block_tiles, KT * TILE + TXT)
    local_keys = key_rows.reshape(shard_tiles, TILE, feature_width)
    local_values = value_rows.reshape(shard_tiles, TILE, feature_width)

    def build_pool(received):
        got_keys, got_values = received
        return (
            jnp.concatenate(
                [local_keys, got_keys.reshape(groups * MOST, TILE, feature_width)], axis=0
            ),
            jnp.concatenate(
                [local_values, got_values.reshape(groups * MOST, TILE, feature_width)], axis=0
            ),
        )

    def block_rows(pool, slot_blk, text_part):
        picked = pool[slot_blk].reshape(block_tiles, KT * TILE, head_count, HD)
        return jnp.concatenate(
            [picked, jnp.broadcast_to(text_part[None], (block_tiles, TXT, head_count, HD))], axis=1
        )

    pool_keys, pool_values = build_pool(
        (
            lax.all_to_all(send_keys, "seq", split_axis=0, concat_axis=0, tiled=True),
            lax.all_to_all(send_values, "seq", split_axis=0, concat_axis=0, tiled=True),
        )
    )
    start = (
        jnp.zeros((pool_size, TILE, feature_width), jnp.float32),
        jnp.zeros((pool_size, TILE, feature_width), jnp.float32),
        jnp.zeros((TXT, head_count, HD), jnp.float32),
        jnp.zeros((TXT, head_count, HD), jnp.float32),
    )

    def forward_step(running, inputs):
        query_blk, grad_blk, slot_blk, live_blk = inputs
        key_blk = block_rows(pool_keys, slot_blk, text_key3)
        value_blk = block_rows(pool_values, slot_blk, text_value3)
        scores, log_total = block_scores(query_blk, key_blk, live_blk, factor)
        output, offset = block_forward(scores, log_total, value_blk, grad_blk)
        return (running, (output.astype(jnp.bfloat16), log_total, offset))

    unused, forwards = lax.scan(
        forward_step, None, (query_blocks, grad_blocks, slot_blocks, live_blocks)
    )
    attended_blocks, total_blocks, offset_blocks = forwards
    again_keys, again_values = build_pool(
        (
            lax.all_to_all(send_keys, "seq", split_axis=0, concat_axis=0, tiled=True),
            lax.all_to_all(send_values, "seq", split_axis=0, concat_axis=0, tiled=True),
        )
    )

    def backward_step(running, inputs):
        key_acc, value_acc, text_key_acc, text_value_acc = running
        query_blk, grad_blk, slot_blk, live_blk, log_total, offset = inputs
        key_blk = block_rows(again_keys, slot_blk, text_key3)
        value_blk = block_rows(again_values, slot_blk, text_value3)
        scores, unused_total = block_scores(query_blk, key_blk, live_blk, factor)
        query_grad, key_grad, value_grad = block_backward(
            scores, log_total, offset, query_blk, key_blk, value_blk, grad_blk, factor
        )
        key_acc, text_key_acc = spread_grads(key_acc, text_key_acc, key_grad, slot_blk)
        value_acc, text_value_acc = spread_grads(value_acc, text_value_acc, value_grad, slot_blk)
        return ((key_acc, value_acc, text_key_acc, text_value_acc), query_grad.astype(jnp.bfloat16))

    finals, query_grad_blocks = lax.scan(
        backward_step,
        start,
        (query_blocks, grad_blocks, slot_blocks, live_blocks, total_blocks, offset_blocks),
    )
    key_acc, value_acc, text_key_acc, text_value_acc = finals
    back_keys, back_values = (
        lax.all_to_all(
            key_acc[shard_tiles:].reshape(groups, MOST * TILE, feature_width),
            "seq",
            split_axis=0,
            concat_axis=0,
            tiled=True,
        ),
        lax.all_to_all(
            value_acc[shard_tiles:].reshape(groups, MOST * TILE, feature_width),
            "seq",
            split_axis=0,
            concat_axis=0,
            tiled=True,
        ),
    )
    out_flat = outgoing.reshape(groups * MOST, shard_tiles)
    target_tile = jnp.where(
        jnp.any(out_flat, axis=1),
        jnp.sum(jnp.where(out_flat, jnp.arange(shard_tiles, dtype=jnp.int32)[None, :], 0), axis=1),
        shard_tiles,
    )
    own_key_grad = (
        key_acc[:shard_tiles]
        .at[target_tile]
        .add(back_keys.reshape(groups * MOST, TILE, feature_width), mode="drop")
    )
    own_value_grad = (
        value_acc[:shard_tiles]
        .at[target_tile]
        .add(back_values.reshape(groups * MOST, TILE, feature_width), mode="drop")
    )
    key_rows3 = key_rows.reshape(token_rows, head_count, HD)
    value_rows3 = value_rows.reshape(token_rows, head_count, HD)
    text_query32 = text_query3.astype(jnp.float32)
    text_key32 = text_key3.astype(jnp.float32)
    text_value32 = text_value3.astype(jnp.float32)
    text_grad32 = text_grad3.astype(jnp.float32)
    video_scores = (
        jnp.einsum("thd,khd->htk", text_query3, key_rows3, preferred_element_type=jnp.float32)
        * factor
    )
    text_scores = (
        jnp.einsum("thd,khd->htk", text_query3, text_key3, preferred_element_type=jnp.float32)
        * factor
    )
    text_scores = jnp.where(text_ok[None, None, :], text_scores, NEGATIVE)
    maximum = jnp.maximum(
        lax.pmax(jnp.max(video_scores, axis=-1), "seq"), jnp.max(text_scores, axis=-1)
    )
    video_exp = jnp.exp(video_scores - maximum[..., None])
    denominator, numerator = lax.psum(
        (jnp.sum(video_exp, axis=-1), split_product("htk,khd->thd", video_exp, value_rows3)), "seq"
    )
    text_exp = jnp.exp(text_scores - maximum[..., None])
    denominator = denominator + jnp.sum(text_exp, axis=-1)
    numerator = numerator + jnp.einsum(
        "htk,khd->thd", text_exp, text_value32, precision=HIGHEST_PRECISION
    )
    log_total = maximum + jnp.log(denominator)
    text_out = numerator / denominator.T[:, :, None]
    video_prob = jnp.exp(video_scores - log_total[..., None])
    text_prob = jnp.exp(text_scores - log_total[..., None])
    text_offset = jnp.sum(text_grad32 * text_out, axis=-1).T
    video_dscore = video_prob * (
        jnp.einsum("thd,khd->htk", text_grad3, value_rows3, preferred_element_type=jnp.float32)
        - text_offset[..., None]
    )
    text_dscore = text_prob * (
        jnp.einsum("thd,khd->htk", text_grad3, text_value3, preferred_element_type=jnp.float32)
        - text_offset[..., None]
    )
    query_part = split_product("htk,khd->thd", video_dscore, key_rows3) * factor
    video_key_from_text = split_product("htk,thd->khd", video_dscore, text_query3) * factor
    video_value_from_text = split_product("htk,thd->khd", video_prob, text_grad3)
    query_sum, key_sum, value_sum = lax.psum((query_part, text_key_acc, text_value_acc), "seq")
    text_query_grad = (
        query_sum
        + jnp.einsum("htk,khd->thd", text_dscore, text_key32, precision=HIGHEST_PRECISION) * factor
    )
    text_key_grad = (
        key_sum
        + jnp.einsum("htk,thd->khd", text_dscore, text_query32, precision=HIGHEST_PRECISION)
        * factor
    )
    text_value_grad = value_sum + jnp.einsum(
        "htk,thd->khd", text_prob, text_grad32, precision=HIGHEST_PRECISION
    )
    attended_rows = attended_blocks.reshape(token_rows, feature_width)
    query_grad_rows = query_grad_blocks.reshape(token_rows, feature_width)
    key_grad_rows = (
        own_key_grad.reshape(token_rows, feature_width)
        + video_key_from_text.reshape(token_rows, feature_width)
    ).astype(jnp.bfloat16)
    value_grad_rows = (
        own_value_grad.reshape(token_rows, feature_width)
        + video_value_from_text.reshape(token_rows, feature_width)
    ).astype(jnp.bfloat16)
    attended_video, video_query_grad, video_key_grad, video_value_grad = (
        lax.all_to_all(attended_rows, "head", split_axis=0, concat_axis=1, tiled=True),
        lax.all_to_all(query_grad_rows, "head", split_axis=0, concat_axis=1, tiled=True),
        lax.all_to_all(key_grad_rows, "head", split_axis=0, concat_axis=1, tiled=True),
        lax.all_to_all(value_grad_rows, "head", split_axis=0, concat_axis=1, tiled=True),
    )
    return (
        attended_video,
        video_query_grad,
        video_key_grad,
        video_value_grad,
        text_out.reshape(TXT, feature_width).astype(jnp.bfloat16),
        text_query_grad.reshape(TXT, feature_width).astype(jnp.bfloat16),
        text_key_grad.reshape(TXT, feature_width).astype(jnp.bfloat16),
        text_value_grad.reshape(TXT, feature_width).astype(jnp.bfloat16),
    )


def solution(mesh):
    placed = (
        P(("seq", "head"), None),
        P(("seq", "head"), None),
        P(("seq", "head"), None),
        P(("seq", "head"), None),
        P(None, "head"),
        P(None, "head"),
        P(None, "head"),
        P(None, "head"),
        P(),
        P(),
        P(),
    )
    return jax.shard_map(
        body,
        mesh=mesh,
        in_specs=placed,
        out_specs=(
            P(("seq", "head"), None),
            P(("seq", "head"), None),
            P(("seq", "head"), None),
            P(("seq", "head"), None),
            P(None, "head"),
            P(None, "head"),
            P(None, "head"),
            P(None, "head"),
        ),
        check_vma=False,
    )
```

profile of v0, /device:TPU:0, one launch (start us, length us, event | category | flops | bytes accessed | tf_op | source)
XLA Modules:
  0.0 900.4 jit_solution(9937720170638479781)
XLA Ops:
  50.8 66.3 %all-to-all-done.1 = bf16[8,256,768]{2,1,0:T(8,128)(2,1)} async-done(((bf16[8,256,768]{2,1,0:T(8,128)(2,1)}), bf16[8,256,768]{2,1,0:T(8,128)(2,1)}, u32[]{:S(2)}, u32[]{:S(2)}) %all-to-all-start.1) | async-done | bytes 3145760 | tf_op jit(solution)/shard_map/all_to_all | solution.py:183
  124.7 67.4 %all-to-all-done.3 = bf16[8,256,768]{2,1,0:T(8,128)(2,1)S(1)} async-done(((bf16[8,256,768]{2,1,0:T(8,128)(2,1)}), bf16[8,256,768]{2,1,0:T(8,128)(2,1)S(1)}, u32[]{:S(2)}, u32[]{:S(2)}) %all-to-all-start.3) | async-done | bytes 3145760 | tf_op jit(solution)/shard_map/all_to_all | solution.py:182
  212.1 13.7 %reshape.401 = bf16[4,1024,6,128]{3,2,1,0:T(8,128)(2,1)} reshape(bf16[32,128,768]{2,1,0:T(8,128)(2,1)} %gather_fusion.1) | data formatting | bytes 12582912 | tf_op jit(solution)/shard_map/while/body/eval_jaxpr/reshape | solution.py:175
  243.1 13.7 %reshape.400 = bf16[4,1024,6,128]{3,2,1,0:T(8,128)(2,1)} reshape(bf16[32,128,768]{2,1,0:T(8,128)(2,1)} %gather_fusion) | data formatting | bytes 12582912 | tf_op jit(solution)/shard_map/while/body/eval_jaxpr/reshape | solution.py:175
  256.8 11.5 %copy.380 = bf16[4,1024,6,128]{1,3,2,0:T(8,128)(2,1)} copy(bf16[4,1024,6,128]{3,2,1,0:T(8,128)(2,1)} %reshape.400) | data formatting | bytes 12582912 | tf_op jit(solution)/shard_map/while/body/eval_jaxpr/reshape | solution.py:175
  285.6 10.6 %bitcast_convert_fusion = (bf16[4,128,6,128]{1,3,2,0:T(8,128)(2,1)}, f32[4,6,128,128]{3,2,1,0:T(8,128)S(1)}) fusion(f32[4,6,1280,128]{3,2,1,0:T(8,128)} %copy-done.2, f32[4,6,128]{2,1,0:T(8,128)S(1)} %log_add_fusion, pred[4,1280]{1,0:T(4,128)(4,1)S(1)} %pad_add_fusion, bf16[4,256,6,128]{1,3,2,0:T(8,128)(2,1)S(1)} %broadcast_in_dim.182, ...), kind=kOutput, calls=%fused_computation.44 | convolution fusion | flops 1038483456 | bytes 25969664 | tf_op jit(solution)/shard_map/while/body/eval_jaxpr/bhtk,bkhd->bthd/dot_general | solution.py:36
  300.9 13.0 %fusion = bf16[4,6,128,1280]{2,3,1,0:T(8,128)(2,1)} fusion(f32[4,6,1280,128]{3,2,1,0:T(8,128)} %copy-done.2, bf16[4,128,6,128]{1,3,2,0:T(8,128)(2,1)S(1)} %bitcast.180, f32[4,6,128]{2,1,0:T(8,128)S(1)} %bitcast.208, f32[4,6,128]{2,1,0:T(8,128)S(1)} %log_add_fusion, pred[4,1280]{1,0:T(4,128)(4,1)S(1)} %pad_add_fusion, ...), kind=kOutput, calls=%fused_computation.9 | convolution fusion | flops 1045954560 | bytes 32273408 | tf_op jit(solution)/shard_map/while/body/eval_jaxpr/bthd,bkhd->bhtk/dot_general | solution.py:44
  326.8 11.1 %convolution_bitcast_fusion = f32[4,1280,6,128]{3,1,2,0:T(8,128)} fusion(bf16[4,128,6,128]{1,3,2,0:T(8,128)(2,1)S(1)} %bitcast.181, f32[4,6,1280,128]{3,2,1,0:T(8,128)} %copy-done.2, f32[4,6,128]{2,1,0:T(8,128)S(1)} %log_add_fusion, pred[4,1280]{1,0:T(4,128)(4,1)S(1)} %pad_add_fusion), kind=kOutput, calls=%fused_computation.19 | convolution fusion | flops 1022361600 | bytes 32261120 | tf_op jit(solution)/shard_map/while/body/eval_jaxpr/bhtk,bthd->bkhd/dot_general | solution.py:56
  337.9 10.4 %slice.43 = f32[4,1024,6,128]{3,1,2,0:T(8,128)} slice(f32[4,1280,6,128]{3,1,2,0:T(8,128)} %convolution_bitcast_fusion), slice={[0:4], [0:1024], [0:6], [0:128]} | slice | bytes 25165824 | tf_op jit(solution)/shard_map/while/body/eval_jaxpr/slice | solution.py:64
  348.3 17.8 %copy.498 = f32[4,1024,6,128]{3,2,1,0:T(8,128)} copy(f32[4,1024,6,128]{3,1,2,0:T(8,128)} %slice.43) | data formatting | bytes 25165824 | tf_op jit(solution)/shard_map/while/body/eval_jaxpr/reshape | solution.py:64
  366.1 16.1 %reshape.404 = f32[32,128,768]{2,1,0:T(8,128)} reshape(f32[4,1024,6,128]{3,2,1,0:T(8,128)} %copy.498) | data formatting | bytes 25165824 | tf_op jit(solution)/shard_map/while/body/eval_jaxpr/reshape | solution.py:64
  386.1 30.2 %scatter_fusion.2 = f32[20,128,768]{2,1,0:T(8,128)} fusion(f32[20,128,768]{2,1,0:T(8,128)} %broadcast.165.clone.1, s32[32]{0:T(128)S(1)} %reshape.345, f32[32,128,768]{2,1,0:T(8,128)} %reshape.404), kind=kCustom, calls=%fused_computation.4 | custom fusion | flops 3145728 | bytes 37748864 | tf_op jit(solution)/shard_map/while/body/eval_jaxpr/scatter-add | solution.py:66
  428.1 11.1 %multiply_bitcast_fusion = f32[4,1280,6,128]{3,1,2,0:T(8,128)} fusion(bf16[4,6,128,1280]{2,3,1,0:T(8,128)(2,1)} %fusion, bf16[4,128,6,128]{1,3,2,0:T(8,128)(2,1)} %bitcast.14), kind=kOutput, calls=%fused_computation.16 | convolution fusion | flops 1010565120 | bytes 24379392 | tf_op jit(solution)/shard_map/while/body/eval_jaxpr/bhtk,bthd->bkhd/dot_general | solution.py:53
  439.2 10.4 %slice.40 = f32[4,1024,6,128]{3,1,2,0:T(8,128)} slice(f32[4,1280,6,128]{3,1,2,0:T(8,128)} %multiply_bitcast_fusion), slice={[0:4], [0:1024], [0:6], [0:128]} | slice | bytes 25165824 | tf_op jit(solution)/shard_map/while/body/eval_jaxpr/slice | solution.py:64
  449.6 17.8 %copy.496 = f32[4,1024,6,128]{3,2,1,0:T(8,128)} copy(f32[4,1024,6,128]{3,1,2,0:T(8,128)} %slice.40) | data formatting | bytes 25165824 | tf_op jit(solution)/shard_map/while/body/eval_jaxpr/reshape | solution.py:64
  467.5 16.1 %reshape.402 = f32[32,128,768]{2,1,0:T(8,128)} reshape(f32[4,1024,6,128]{3,2,1,0:T(8,128)} %copy.496) | data formatting | bytes 25165824 | tf_op jit(solution)/shard_map/while/body/eval_jaxpr/reshape | solution.py:64
  487.5 30.1 %scatter_fusion = f32[20,128,768]{2,1,0:T(8,128)} fusion(f32[20,128,768]{2,1,0:T(8,128)} %broadcast.165.clone, s32[32]{0:T(128)S(1)} %reshape.345, f32[32,128,768]{2,1,0:T(8,128)} %reshape.402), kind=kCustom, calls=%fused_computation.2 | custom fusion | flops 3145728 | bytes 37748864 | tf_op jit(solution)/shard_map/while/body/eval_jaxpr/scatter-add | solution.py:66
  523.7 43.3 %all-to-all-done.10 = f32[8,256,768]{2,1,0:T(8,128)} async-done(((f32[8,256,768]{2,1,0:T(8,128)}), f32[8,256,768]{2,1,0:T(8,128)}, u32[]{:S(2)}, u32[]{:S(2)}) %all-to-all-start.10) | async-done | bytes 6291488 | tf_op jit(solution)/shard_map/all_to_all | solution.py:239
  583.2 103.5 %pmax.7 = f32[6,256]{1,0:T(8,128)} all-reduce(f32[6,256]{1,0:T(8,128)S(1)} %get-tuple-element.153), channel_id=1, replica_groups=mesh['seq'=8,'head'=4] {'seq'}, use_global_device_ids=true, to_apply=%region_12.13 | all-reduce | flops 1536 | bytes 12288 | tf_op jit(solution)/shard_map/pmax | solution.py:279
  692.2 44.9 %psum.35 = f32[6,256]{1,0:T(8,128)} all-reduce(f32[6,256]{1,0:T(8,128)S(1)} %fusion.9), channel_id=1, replica_groups=mesh['seq'=8,'head'=4] {'seq'}, use_global_device_ids=true, to_apply=%region_15.16 | all-reduce | flops 1536 | bytes 12288 | tf_op jit(solution)/shard_map/psum | solution.py:282
  747.5 32.2 %all-reduce.4.cloned.1.call-done = f32[256,6,128]{2,0,1:T(8,128)} async-done(((f32[256,6,128]{2,0,1:T(8,128)}), f32[256,6,128]{2,0,1:T(8,128)}) %all-reduce.4.cloned.1.call-update) | async-done | bytes 786448 | tf_op jit(solution)/shard_map/psum | solution.py:282
  812.2 9.2 %scatter_fusion.3 = f32[4,128,768]{2,1,0:T(8,128)S(1)} fusion(f32[4,128,768]{2,1,0:T(8,128)S(1)} %slice_add_fusion, s32[16]{0:T(128)S(1)} %copy-done.35, f32[16,128,768]{2,1,0:T(8,128)} %bitcast.47), kind=kCustom, calls=%fused_computation.5 | custom fusion | flops 1572864 | bytes 18874432 | tf_op jit(solution)/shard_map/scatter-add | solution.py:261
  833.5 29.9 %all-reduce.6.cloned.1.call-done = (f32[256,6,128]{2,0,1:T(8,128)}, f32[256,6,128]{2,0,1:T(8,128)}, f32[256,6,128]{0,2,1:T(8,128)}) async-done(((f32[256,6,128]{2,0,1:T(8,128)}, f32[256,6,128]{2,0,1:T(8,128)}, f32[256,6,128]{0,2,1:T(8,128)}), (f32[256,6,128]{2,0,1:T(8,128)}, f32[256,6,128]{2,0,1:T(8,128)}, f32[256,6,128]{0,2,1:T(8,128)})) %all-reduce.6.cloned.1.call-update) | async-done | bytes 2359312 | tf_op jit(solution)/shard_map/psum | solution.py:306
  868.4 9.2 %scatter_fusion.1 = f32[4,128,768]{2,1,0:T(8,128)S(1)} fusion(f32[4,128,768]{2,1,0:T(8,128)S(1)} %slice_add_fusion.1, s32[16]{0:T(128)S(1)} %copy-done.35, f32[16,128,768]{2,1,0:T(8,128)} %bitcast.41), kind=kCustom, calls=%fused_computation.3 | custom fusion | flops 1572864 | bytes 18874432 | tf_op jit(solution)/shard_map/scatter-add | solution.py:256
  (228 shorter events, 245.9 us)
Async XLA Ops:
  7.2 8.0 copy-start.33
  7.2 8.0 copy-start.38
  7.2 8.4 copy-start.26
  9.9 16.0 %all-to-all-start = ((bf16[128,4,768]{2,0,1:T(8,128)(2,1)}), bf16[128,4,768]{2,0,1:T(8,128)(2,1)S(1)}, u32[]{:S(2)}, u32[]{:S(2)}) async-start(bf16[128,4,768]{2,0,1:T(8,128)(2,1)} %copy.369), calls=%async_computation | async-start | bytes 1572864 | tf_op jit(solution)/shard_map/all_to_all | solution.py:90
  26.0 14.6 %all-to-all-start.2 = ((bf16[128,4,768]{2,0,1:T(8,128)(2,1)}), bf16[128,4,768]{2,0,1:T(8,128)(2,1)}, u32[]{:S(2)}, u32[]{:S(2)}) async-start(bf16[128,4,768]{2,0,1:T(8,128)(2,1)} %copy.382), calls=%async_computation.2 | async-start | bytes 1572864 | tf_op jit(solution)/shard_map/all_to_all | solution.py:89
  30.4 91.1 %copy-start.29 = (pred[8,8,2,4]{1,3,2,0:T(4,128)(4,1)}, pred[8,8,2,4]{1,3,2,0:T(4,128)(4,1)S(1)}, u32[]{:S(2)}) copy-start(pred[8,8,2,4]{1,3,2,0:T(4,128)(4,1)S(1)} %fusion.48) | copy-start | bytes 1540
  40.6 76.5 %all-to-all-start.1 = ((bf16[8,256,768]{2,1,0:T(8,128)(2,1)}), bf16[8,256,768]{2,1,0:T(8,128)(2,1)}, u32[]{:S(2)}, u32[]{:S(2)}) async-start(bf16[8,256,768]{2,1,0:T(8,128)(2,1)} %reshape.323), calls=%async_computation.1 | async-start | bytes 6291456 | tf_op jit(solution)/shard_map/all_to_all | solution.py:183
  50.8 70.0 %copy-start.39 = (s32[256]{0:T(256)S(1)}, s32[256]{0:T(256)}, u32[]{:S(2)}) copy-start(s32[256]{0:T(256)} %param.21) | copy-start | bytes 3076
  117.1 75.1 %all-to-all-start.3 = ((bf16[8,256,768]{2,1,0:T(8,128)(2,1)}), bf16[8,256,768]{2,1,0:T(8,128)(2,1)S(1)}, u32[]{:S(2)}, u32[]{:S(2)}) async-start(bf16[8,256,768]{2,1,0:T(8,128)(2,1)} %reshape.328), calls=%async_computation.3 | async-start | bytes 6291456 | tf_op jit(solution)/shard_map/all_to_all | solution.py:182
  192.2 76.1 %all-to-all-start.4 = ((bf16[128,4,768]{0,2,1:T(8,128)(2,1)}), bf16[128,4,768]{0,2,1:T(8,128)(2,1)}, u32[]{:S(2)}, u32[]{:S(2)}) async-start(bf16[128,4,768]{0,2,1:T(8,128)(2,1)} %bitcast.192), calls=%async_computation.4 | async-start | bytes 1572864 | tf_op jit(solution)/shard_map/all_to_all | solution.py:88
  197.8 8.5 copy-start.15
  225.7 7.5 copy-start.12
  256.8 15.7 %copy-start.25 = (bf16[256,6,128]{2,0,1:T(8,128)(2,1)S(1)}, bf16[256,6,128]{2,0,1:T(8,128)(2,1)}, u32[]{:S(2)}) copy-start(bf16[256,6,128]{2,0,1:T(8,128)(2,1)} %copy.385) | copy-start | bytes 1179652
  268.3 27.9 %all-to-all-start.6 = ((bf16[128,4,768]{0,2,1:T(8,128)(2,1)}), bf16[128,4,768]{0,2,1:T(8,128)(2,1)S(1)}, u32[]{:S(2)}, u32[]{:S(2)}) async-start(bf16[128,4,768]{0,2,1:T(8,128)(2,1)} %bitcast.20), calls=%async_computation.6 | async-start | bytes 1572864 | tf_op jit(solution)/shard_map/all_to_all | solution.py:91
  296.2 26.0 %all-to-all-start.5 = ((bf16[4,128,768]{1,2,0:T(8,128)(2,1)}), bf16[4,128,768]{1,2,0:T(8,128)(2,1)S(1)}, u32[]{:S(2)}, u32[]{:S(2)}) async-start(bf16[4,128,768]{1,2,0:T(8,128)(2,1)} %bitcast.203), calls=%async_computation.5 | async-start | bytes 1572864 | tf_op jit(solution)/shard_map/all_to_all | solution.py:330
  300.8 13.0 %copy-start.23 = (bf16[4,256,6,128]{3,1,2,0:T(8,128)(2,1)S(1)}, bf16[4,256,6,128]{3,1,2,0:T(8,128)(2,1)}, u32[]{:S(2)}) copy-start(bf16[4,256,6,128]{3,1,2,0:T(8,128)(2,1)} %copy-done.22) | copy-start | bytes 4718596
  322.2 15.7 %copy-start.20 = (bf16[4,128,768]{1,2,0:T(8,128)(2,1)}, bf16[4,128,768]{1,2,0:T(8,128)(2,1)S(1)}, u32[]{:S(2)}) copy-start(bf16[4,128,768]{1,2,0:T(8,128)(2,1)S(1)} %all-to-all-done.5) | copy-start | bytes 2359300
  322.2 100.2 %all-to-all-start.7 = ((bf16[4,128,768]{1,2,0:T(8,128)(2,1)}), bf16[4,128,768]{1,2,0:T(8,128)(2,1)S(1)}, u32[]{:S(2)}, u32[]{:S(2)}) async-start(bf16[4,128,768]{1,2,0:T(8,128)(2,1)} %bitcast.202), calls=%async_computation.7 | async-start | bytes 1572864 | tf_op jit(solution)/shard_map/all_to_all | solution.py:331
  423.4 143.7 %all-to-all-start.10 = ((f32[8,256,768]{2,1,0:T(8,128)}), f32[8,256,768]{2,1,0:T(8,128)}, u32[]{:S(2)}, u32[]{:S(2)}) async-start(f32[8,256,768]{2,1,0:T(8,128)} %bitcast.163), calls=%async_computation.10 | async-start | bytes 12582912 | tf_op jit(solution)/shard_map/all_to_all | solution.py:239
  567.1 255.4 %all-to-all-start.8 = ((f32[8,256,768]{2,1,0:T(8,128)}), f32[8,256,768]{2,1,0:T(8,128)}, u32[]{:S(2)}, u32[]{:S(2)}) async-start(f32[8,256,768]{2,1,0:T(8,128)} %bitcast.162), calls=%async_computation.8 | async-start | bytes 12582912 | tf_op jit(solution)/shard_map/all_to_all | solution.py:232
  572.0 207.6 %all-reduce.4.cloned.1.call-start = ((), (), s32[]{:S(2)}) async-start(), calls=%async_computation.12 | async-start | bytes 1572864 | tf_op jit(solution)/shard_map/psum | solution.py:282
  691.2 172.3 %all-reduce.6.cloned.1.call-start = ((), (), s32[]{:S(2)}) async-start(), calls=%async_computation.13 | async-start | bytes 4718592 | tf_op jit(solution)/shard_map/psum | solution.py:306
  822.4 56.1 %all-to-all-start.11 = ((bf16[4,128,768]{2,1,0:T(8,128)(2,1)}), bf16[4,128,768]{2,1,0:T(8,128)(2,1)}, u32[]{:S(2)}, u32[]{:S(2)}) async-start(bf16[4,128,768]{2,1,0:T(8,128)(2,1)} %convert_element_type.127), calls=%async_computation.11 | async-start | bytes 1572864 | tf_op jit(solution)/shard_map/all_to_all | solution.py:333
  878.5 13.3 %all-to-all-start.9 = ((bf16[4,128,768]{2,1,0:T(8,128)(2,1)}), bf16[4,128,768]{2,1,0:T(8,128)(2,1)S(1)}, u32[]{:S(2)}, u32[]{:S(2)}) async-start(bf16[4,128,768]{2,1,0:T(8,128)(2,1)} %convert_element_type.123), calls=%async_computation.9 | async-start | bytes 1572864 | tf_op jit(solution)/shard_map/all_to_all | solution.py:332
  (30 other events, 130.1 us)
Sparse Core Ops, SparseCore 0:
  691.3 88.3 all-reduce.3
  797.1 66.2 all-reduce.5
where the time goes:
time: 911 us; the launch traced here: 900 us
  waiting for transfers between devices  253 us (28%)
  local copies, waits for them, and re-layouts  228 us (25%)
  blocking collectives  148 us (16%)
  other arithmetic  109 us (12%)
  matrix products  94.3 us (10%)
  starting transfers between devices  53.4 us (6%)
  between operations  14.9 us (2%)
    pmax x1, blocking collectives, body(): lax.pmax(jnp.max(video_scores, axis=-1), 'seq')  104 us
    reshape x4, local copies, waits for them, and re-layouts, spread_grads(): grad_blk[:, :KT * TILE].reshape(block_tiles, KT, TILE, pool_total.shape[2])  67.9 us
    all_to_all x1, waiting for transfers between devices, body(): lax.all_to_all(send_keys, 'seq', split_axis=0, concat_axis=0, tiled=True)  67.4 us
    all_to_all x1, waiting for transfers between devices, body(): lax.all_to_all(send_values, 'seq', split_axis=0, concat_axis=0, tiled=True)  66.3 us
    scatter-add x2, other arithmetic, spread_grads(): pool_total.at[pool_slot].add(tile_part)  60.3 us
    reshape x4, local copies, waits for them, and re-layouts, block_rows(): picked = pool[slot_blk].reshape(block_tiles, KT * TILE, head_count, HD)  46.3 us
    psum x1, blocking collectives, body(): lax.psum((jnp.sum(video_exp, axis=-1), split_product('htk,khd->thd', vide...  44.9 us
    all_to_all x1, waiting for transfers between devices, body(): lax.all_to_all(value_acc[shard_tiles:].reshape(groups, MOST * TILE, featu...  43.3 us
  transfers between devices with their start and end apart: 14, of which 8 were waited for; matrix products, arithmetic and copies ran while one was open for 47% of the time, Pallas kernels for 0%

commit v1 on v0

--- a/solution.py
+++ b/solution.py
@@ -10,6 +10,18 @@
 MOST = 2
 NEGATIVE = -1e30
 HIGHEST_PRECISION = lax.Precision.HIGHEST
+
+
+def sent_to_each(value, axis, split, join):
+    ways, here = (lax.axis_size(axis), lax.axis_index(axis))
+    width = value.shape[split] // ways
+    turned = jnp.roll(value, -here * width, axis=split)
+    got = [lax.slice_in_dim(turned, 0, width, axis=split)]
+    for far in range(1, ways):
+        sent = lax.slice_in_dim(turned, far * width, (far + 1) * width, axis=split)
+        got.append(lax.ppermute(sent, axis, [(d, (d + far) % ways) for d in range(ways)]))
+    line = jnp.concatenate(got[::-1], axis=join)
+    return jnp.roll(line, (here + 1) * got[0].shape[join], axis=join)
 
 
 def split_product(form, weights, data):
@@ -180,7 +192,7 @@
     pool_keys, pool_values = build_pool(
         (
             lax.all_to_all(send_keys, "seq", split_axis=0, concat_axis=0, tiled=True),
-            lax.all_to_all(send_values, "seq", split_axis=0, concat_axis=0, tiled=True),
+            sent_to_each(send_values, "seq", 0, 0),
         )
     )
     start = (

time: 911 us -> 1020 us (1.12)
  starting transfers between devices: 53.4 us -> 129 us
  local copies, waits for them, and re-layouts: 228 us -> 268 us
  waiting for transfers between devices: 253 us -> 225 us
    ppermute x0 -> x7, starting transfers between devices: none -> 76 us  [sent_to_each(): lax.ppermute(sent, axis, [(d, (d + far) % ways) for d in range(ways)])]
    all_to_all x1, waiting for transfers between devices: 67.4 us -> 0.01 us  [body(): lax.all_to_all(send_keys, 'seq', split_axis=0, concat_axis=0, tiled=True)]
    ppermute x0 -> x7, waiting for transfers between devices: none -> 44.4 us  [sent_to_each(): lax.ppermute(sent, axis, [(d, (d + far) % ways) for d in range(ways)])]
    reshape x4 -> x6, local copies, waits for them, and re-layouts: 46.3 us -> 67.5 us  [block_rows(): picked = pool[slot_blk].reshape(block_tiles, KT * TILE, head_count, HD)]
    unnamed x98 -> x116, local copies, waits for them, and re-layouts: 23.1 us -> 28.3 us
  transfers between devices with their start and end apart: 14 -> 21, of which waited for: 8 -> 9; matrix products, arithmetic and copies ran while one was open for 47% -> 47% of each run, Pallas kernels for 0% -> 0%
where the time goes in v1:
time: 1020 us; the launch traced here: 1010 us
  local copies, waits for them, and re-layouts  268 us (26%)
  waiting for transfers between devices  225 us (22%)
  blocking collectives  149 us (15%)
  starting transfers between devices  129 us (13%)
  other arithmetic  119 us (12%)
  matrix products  100 us (10%)
  between operations  15 us (1%)
    pmax x1, blocking collectives, body(): lax.pmax(jnp.max(video_scores, axis=-1), 'seq')  104 us
    ppermute x7, starting transfers between devices, sent_to_each(): lax.ppermute(sent, axis, [(d, (d + far) % ways) for d in range(ways)])  76 us
    reshape x4, local copies, waits for them, and re-layouts, spread_grads(): grad_blk[:, :KT * TILE].reshape(block_tiles, KT, TILE, pool_total.shape[2])  67.9 us
    reshape x6, local copies, waits for them, and re-layouts, block_rows(): picked = pool[slot_blk].reshape(block_tiles, KT * TILE, head_count, HD)  67.5 us
    all_to_all x1, waiting for transfers between devices, body(): lax.all_to_all(send_values, 'seq', split_axis=0, concat_axis=0, tiled=True)  64.4 us
    scatter-add x2, other arithmetic, spread_grads(): pool_total.at[pool_slot].add(tile_part)  60.4 us
    psum x1, blocking collectives, body(): lax.psum((jnp.sum(video_exp, axis=-1), split_product('htk,khd->thd', vide...  44.8 us
    ppermute x7, waiting for transfers between devices, sent_to_each(): lax.ppermute(sent, axis, [(d, (d + far) % ways) for d in range(ways)])  44.4 us
  transfers between devices with their start and end apart: 21, of which 9 were waited for; matrix products, arithmetic and copies ran while one was open for 47% of the time, Pallas kernels for 0%

profile of v1, /device:TPU:0, one launch (start us, length us, event | category | flops | bytes accessed | tf_op | source)
XLA Modules:
  0.0 1005.4 jit_solution(2588712281314268306)
XLA Ops:
  51.9 64.4 %all-to-all-done.5 = bf16[8,256,768]{2,1,0:T(8,128)(2,1)} async-done(((bf16[8,256,768]{2,1,0:T(8,128)(2,1)}), bf16[8,256,768]{2,1,0:T(8,128)(2,1)}, u32[]{:S(2)}, u32[]{:S(2)}) %all-to-all-start.5) | async-done | bytes 3145760 | tf_op jit(solution)/shard_map/all_to_all | solution.py:220
  140.5 40.7 %collective-permute-done = bf16[1,256,768]{2,1,0:T(8,128)(2,1)} collective-permute-done((bf16[1,256,768]{2,1,0:T(8,128)(2,1)}, bf16[1,256,768]{2,1,0:T(8,128)(2,1)}, u32[]{:S(2)}, u32[]{:S(2)}) %collective-permute-start) | collective-permute-done | bytes 393248 | tf_op jit(solution)/shard_map/ppermute | solution.py:22
  181.1 45.4 %collective-permute-start.4 = (bf16[1,256,768]{2,1,0:T(8,128)(2,1)}, bf16[1,256,768]{2,1,0:T(8,128)(2,1)S(1)}, u32[]{:S(2)}, u32[]{:S(2)}) collective-permute-start(bf16[1,256,768]{2,1,0:T(8,128)(2,1)} %get-tuple-element.148), channel_id=1, source_target_pairs={{0,12},{4,16},{8,20},{12,24},{16,28},{20,0},{24,4},{28,8},{1,13},{... | collective-permute-start | bytes 1179656 | tf_op jit(solution)/shard_map/ppermute | solution.py:22
  228.3 24.0 %collective-permute-start.5 = (bf16[1,256,768]{2,1,0:T(8,128)(2,1)}, bf16[1,256,768]{2,1,0:T(8,128)(2,1)S(1)}, u32[]{:S(2)}, u32[]{:S(2)}) collective-permute-start(bf16[1,256,768]{2,1,0:T(8,128)(2,1)} %get-tuple-element.147), channel_id=1, source_target_pairs={{0,8},{4,12},{8,16},{12,20},{16,24},{20,28},{24,0},{28,4},{1,9},{5... | collective-permute-start | bytes 1179656 | tf_op jit(solution)/shard_map/ppermute | solution.py:22
  283.8 13.7 %reshape.417 = bf16[4,1024,6,128]{3,2,1,0:T(8,128)(2,1)} reshape(bf16[32,128,768]{2,1,0:T(8,128)(2,1)} %gather_fusion.1) | data formatting | bytes 12582912 | tf_op jit(solution)/shard_map/while/body/eval_jaxpr/reshape | solution.py:187
  315.7 13.7 %reshape.416 = bf16[4,1024,6,128]{3,2,1,0:T(8,128)(2,1)} reshape(bf16[32,128,768]{2,1,0:T(8,128)(2,1)} %gather_fusion) | data formatting | bytes 12582912 | tf_op jit(solution)/shard_map/while/body/eval_jaxpr/reshape | solution.py:187
  329.3 11.5 %copy.389 = bf16[4,1024,6,128]{1,3,2,0:T(8,128)(2,1)} copy(bf16[4,1024,6,128]{3,2,1,0:T(8,128)(2,1)} %reshape.416) | data formatting | bytes 12582912 | tf_op jit(solution)/shard_map/while/body/eval_jaxpr/reshape | solution.py:187
  360.8 10.9 %bitcast_convert_fusion = (bf16[4,128,6,128]{1,3,2,0:T(8,128)(2,1)}, f32[4,6,128,128]{3,2,1,0:T(8,128)}) fusion(f32[4,6,1280,128]{3,2,1,0:T(8,128)} %copy-done.2, f32[4,6,128]{2,1,0:T(8,128)S(1)} %log_add_fusion, pred[4,1280]{1,0:T(4,128)(4,1)S(1)} %pad_add_fusion, bf16[4,256,6,128]{1,3,2,0:T(8,128)(2,1)S(1)} %broadcast_in_dim.182, ...), kind=kOutput, calls=%fused_computation.57 | convolution fusion | flops 1038483456 | bytes 25969664 | tf_op jit(solution)/shard_map/while/body/eval_jaxpr/bhtk,bkhd->bthd/dot_general | solution.py:48
  377.4 13.7 %reshape.418 = bf16[4,1024,6,128]{3,2,1,0:T(8,128)(2,1)} reshape(bf16[32,128,768]{2,1,0:T(8,128)(2,1)} %gather_fusion.2) | data formatting | bytes 12582912 | tf_op jit(solution)/shard_map/while/body/eval_jaxpr/reshape | solution.py:187
  406.0 12.2 %fusion = bf16[4,6,128,1280]{2,3,1,0:T(8,128)(2,1)} fusion(f32[4,6,1280,128]{3,2,1,0:T(8,128)} %copy-done.2, bf16[4,128,6,128]{1,3,2,0:T(8,128)(2,1)S(1)} %bitcast.186, bf16[4,256,6,128]{3,1,2,0:T(8,128)(2,1)} %broadcast_in_dim.182.clone, bf16[4,1024,6,128]{3,1,2,0:T(8,128)(2,1)} %copy.401, f32[4,6,128]{2,1,0:T(8,128)S(1)} %bitcast.216, ...), kind=kOutput, calls=%fused_computation.10 | convolution fusion | flops 1045954560 | bytes 32273408 | tf_op jit(solution)/shard_map/while/body/eval_jaxpr/bthd,bkhd->bhtk/dot_general | solution.py:56
  431.8 11.1 %convolution_bitcast_fusion = f32[4,1280,6,128]{3,1,2,0:T(8,128)} fusion(bf16[4,128,6,128]{1,3,2,0:T(8,128)(2,1)S(1)} %bitcast.187, f32[4,6,1280,128]{3,2,1,0:T(8,128)} %copy-done.2, f32[4,6,128]{2,1,0:T(8,128)S(1)} %copy-done.35, pred[4,1280]{1,0:T(4,128)(4,1)S(1)} %pad_add_fusion), kind=kOutput, calls=%fused_computation.20 | convolution fusion | flops 1022361600 | bytes 32261120 | tf_op jit(solution)/shard_map/while/body/eval_jaxpr/bhtk,bthd->bkhd/dot_general | solution.py:68
  453.2 17.9 %copy.510 = f32[4,1024,6,128]{3,2,1,0:T(8,128)} copy(f32[4,1024,6,128]{3,1,2,0:T(8,128)} %slice.85) | data formatting | bytes 25165824 | tf_op jit(solution)/shard_map/while/body/eval_jaxpr/reshape | solution.py:76
  471.0 16.0 %reshape.421 = f32[32,128,768]{2,1,0:T(8,128)} reshape(f32[4,1024,6,128]{3,2,1,0:T(8,128)} %copy.510) | data formatting | bytes 25165824 | tf_op jit(solution)/shard_map/while/body/eval_jaxpr/reshape | solution.py:76
  491.0 30.3 %scatter_fusion.2 = f32[20,128,768]{2,1,0:T(8,128)} fusion(f32[20,128,768]{2,1,0:T(8,128)} %broadcast.166.clone.1, s32[32]{0:T(128)S(1)} %reshape.351, f32[32,128,768]{2,1,0:T(8,128)} %reshape.421), kind=kCustom, calls=%fused_computation.5 | custom fusion | flops 3145728 | bytes 37748864 | tf_op jit(solution)/shard_map/while/body/eval_jaxpr/scatter-add | solution.py:78
  533.1 11.0 %multiply_bitcast_fusion = f32[4,1280,6,128]{3,1,2,0:T(8,128)} fusion(bf16[4,6,128,1280]{2,3,1,0:T(8,128)(2,1)} %fusion, bf16[4,128,6,128]{1,3,2,0:T(8,128)(2,1)S(1)} %bitcast.196), kind=kOutput, calls=%fused_computation.17 | convolution fusion | flops 1010565120 | bytes 24379392 | tf_op jit(solution)/shard_map/while/body/eval_jaxpr/bhtk,bthd->bkhd/dot_general | solution.py:65
  544.1 10.4 %slice.82 = f32[4,1024,6,128]{3,1,2,0:T(8,128)} slice(f32[4,1280,6,128]{3,1,2,0:T(8,128)} %multiply_bitcast_fusion), slice={[0:4], [0:1024], [0:6], [0:128]} | slice | bytes 25165824 | tf_op jit(solution)/shard_map/while/body/eval_jaxpr/slice | solution.py:76
  554.5 17.9 %copy.508 = f32[4,1024,6,128]{3,2,1,0:T(8,128)} copy(f32[4,1024,6,128]{3,1,2,0:T(8,128)} %slice.82) | data formatting | bytes 25165824 | tf_op jit(solution)/shard_map/while/body/eval_jaxpr/reshape | solution.py:76
  572.3 16.1 %reshape.419 = f32[32,128,768]{2,1,0:T(8,128)} reshape(f32[4,1024,6,128]{3,2,1,0:T(8,128)} %copy.508) | data formatting | bytes 25165824 | tf_op jit(solution)/shard_map/while/body/eval_jaxpr/reshape | solution.py:76
  592.4 30.1 %scatter_fusion = f32[20,128,768]{2,1,0:T(8,128)} fusion(f32[20,128,768]{2,1,0:T(8,128)} %broadcast.166.clone, s32[32]{0:T(128)S(1)} %reshape.351, f32[32,128,768]{2,1,0:T(8,128)} %reshape.419), kind=kCustom, calls=%fused_computation.3 | custom fusion | flops 3145728 | bytes 37748864 | tf_op jit(solution)/shard_map/while/body/eval_jaxpr/scatter-add | solution.py:78
  628.6 43.4 %all-to-all-done.10 = f32[8,256,768]{2,1,0:T(8,128)} async-done(((f32[8,256,768]{2,1,0:T(8,128)}), f32[8,256,768]{2,1,0:T(8,128)}, u32[]{:S(2)}, u32[]{:S(2)}) %all-to-all-start.10) | async-done | bytes 6291488 | tf_op jit(solution)/shard_map/all_to_all | solution.py:251
  687.3 104.4 %pmax.7 = f32[6,256]{1,0:T(8,128)} all-reduce(f32[6,256]{1,0:T(8,128)S(1)} %get-tuple-element.163), channel_id=1, replica_groups=mesh['seq'=8,'head'=4] {'seq'}, use_global_device_ids=true, to_apply=%region_12.14 | all-reduce | flops 1536 | bytes 12288 | tf_op jit(solution)/shard_map/pmax | solution.py:291
  797.2 44.8 %psum.35 = f32[6,256]{1,0:T(8,128)} all-reduce(f32[6,256]{1,0:T(8,128)S(1)} %fusion.17), channel_id=1, replica_groups=mesh['seq'=8,'head'=4] {'seq'}, use_global_device_ids=true, to_apply=%region_15.17 | all-reduce | flops 1536 | bytes 12288 | tf_op jit(solution)/shard_map/psum | solution.py:294
  852.4 32.2 %all-reduce.4.cloned.1.call-done = f32[256,6,128]{2,0,1:T(8,128)} async-done(((f32[256,6,128]{2,0,1:T(8,128)}), f32[256,6,128]{2,0,1:T(8,128)}) %all-reduce.4.cloned.1.call-update) | async-done | bytes 786448 | tf_op jit(solution)/shard_map/psum | solution.py:294
  938.6 29.8 %all-reduce.6.cloned.1.call-done = (f32[256,6,128]{2,0,1:T(8,128)}, f32[256,6,128]{2,0,1:T(8,128)}, f32[256,6,128]{0,2,1:T(8,128)}) async-done(((f32[256,6,128]{2,0,1:T(8,128)}, f32[256,6,128]{2,0,1:T(8,128)}, f32[256,6,128]{0,2,1:T(8,128)}), (f32[256,6,128]{2,0,1:T(8,128)}, f32[256,6,128]{2,0,1:T(8,128)}, f32[256,6,128]{0,2,1:T(8,128)})) %all-reduce.6.cloned.1.call-update) | async-done | bytes 2359312 | tf_op jit(solution)/shard_map/psum | solution.py:318
  (268 shorter events, 324.8 us)
Async XLA Ops:
  9.9 16.0 %all-to-all-start = ((bf16[128,4,768]{2,0,1:T(8,128)(2,1)}), bf16[128,4,768]{2,0,1:T(8,128)(2,1)S(1)}, u32[]{:S(2)}, u32[]{:S(2)}) async-start(bf16[128,4,768]{2,0,1:T(8,128)(2,1)} %copy.378), calls=%async_computation | async-start | bytes 1572864 | tf_op jit(solution)/shard_map/all_to_all | solution.py:102
  26.0 279.1 %copy-start.8 = (bf16[128,4,768]{2,0,1:T(8,128)(2,1)}, bf16[128,4,768]{2,0,1:T(8,128)(2,1)S(1)}, u32[]{:S(2)}) copy-start(bf16[128,4,768]{2,0,1:T(8,128)(2,1)S(1)} %all-to-all-done) | copy-start | bytes 2359300
  26.0 13.8 %all-to-all-start.1 = ((bf16[128,4,768]{2,0,1:T(8,128)(2,1)}), bf16[128,4,768]{2,0,1:T(8,128)(2,1)S(1)}, u32[]{:S(2)}, u32[]{:S(2)}) async-start(bf16[128,4,768]{2,0,1:T(8,128)(2,1)} %copy.391), calls=%async_computation.1 | async-start | bytes 1572864 | tf_op jit(solution)/shard_map/all_to_all | solution.py:101
  39.8 234.2 %copy-start.15 = (bf16[128,4,768]{2,0,1:T(8,128)(2,1)}, bf16[128,4,768]{2,0,1:T(8,128)(2,1)S(1)}, u32[]{:S(2)}) copy-start(bf16[128,4,768]{2,0,1:T(8,128)(2,1)S(1)} %all-to-all-done.1) | copy-start | bytes 2359300
  39.8 76.5 %all-to-all-start.5 = ((bf16[8,256,768]{2,1,0:T(8,128)(2,1)}), bf16[8,256,768]{2,1,0:T(8,128)(2,1)}, u32[]{:S(2)}, u32[]{:S(2)}) async-start(bf16[8,256,768]{2,1,0:T(8,128)(2,1)} %reshape.327), calls=%async_computation.5 | async-start | bytes 6291456 | tf_op jit(solution)/shard_map/all_to_all | solution.py:220
  116.3 149.3 %all-to-all-start.2 = ((bf16[8,256,768]{2,1,0:T(8,128)(2,1)}), bf16[8,256,768]{2,1,0:T(8,128)(2,1)}, u32[]{:S(2)}, u32[]{:S(2)}) async-start(bf16[8,256,768]{2,1,0:T(8,128)(2,1)} %reshape.332), calls=%async_computation.2 | async-start | bytes 6291456 | tf_op jit(solution)/shard_map/all_to_all | solution.py:194
  128.6 52.5 %collective-permute-start = (bf16[1,256,768]{2,1,0:T(8,128)(2,1)}, bf16[1,256,768]{2,1,0:T(8,128)(2,1)}, u32[]{:S(2)}, u32[]{:S(2)}) collective-permute-start(bf16[1,256,768]{2,1,0:T(8,128)(2,1)} %get-tuple-element.152), channel_id=1, source_target_pairs={{0,28},{4,0},{8,4},{12,8},{16,12},{20,16},{24,20},{28,24},{1,29},{... | collective-permute-start | bytes 1179656 | tf_op jit(solution)/shard_map/ppermute | solution.py:22
  132.3 121.8 %collective-permute-start.2 = (bf16[1,256,768]{2,1,0:T(8,128)(2,1)}, bf16[1,256,768]{2,1,0:T(8,128)(2,1)}, u32[]{:S(2)}, u32[]{:S(2)}) collective-permute-start(bf16[1,256,768]{2,1,0:T(8,128)(2,1)} %get-tuple-element.150), channel_id=1, source_target_pairs={{0,20},{4,24},{8,28},{12,0},{16,4},{20,8},{24,12},{28,16},{1,21},{... | collective-permute-start | bytes 1179656 | tf_op jit(solution)/shard_map/ppermute | solution.py:22
  132.4 96.0 %collective-permute-start.1 = (bf16[1,256,768]{2,1,0:T(8,128)(2,1)}, bf16[1,256,768]{2,1,0:T(8,128)(2,1)}, u32[]{:S(2)}, u32[]{:S(2)}) collective-permute-start(bf16[1,256,768]{2,1,0:T(8,128)(2,1)} %get-tuple-element.151), channel_id=1, source_target_pairs={{0,24},{4,28},{8,0},{12,4},{16,8},{20,12},{24,16},{28,20},{1,25},{... | collective-permute-start | bytes 1179656 | tf_op jit(solution)/shard_map/ppermute | solution.py:22
  133.3 126.4 %collective-permute-start.3 = (bf16[1,256,768]{2,1,0:T(8,128)(2,1)}, bf16[1,256,768]{2,1,0:T(8,128)(2,1)}, u32[]{:S(2)}, u32[]{:S(2)}) collective-permute-start(bf16[1,256,768]{2,1,0:T(8,128)(2,1)} %get-tuple-element.149), channel_id=1, source_target_pairs={{0,16},{4,20},{8,24},{12,28},{16,0},{20,4},{24,8},{28,12},{1,17},{... | collective-permute-start | bytes 1179656 | tf_op jit(solution)/shard_map/ppermute | solution.py:22
  136.1 224.5 %copy-start.21 = (bf16[256,768]{0,1:T(8,128)(2,1)}, bf16[256,768]{0,1:T(8,128)(2,1)S(1)}, u32[]{:S(2)}) copy-start(bf16[256,768]{0,1:T(8,128)(2,1)S(1)} %copy.388) | copy-start | bytes 1179652
  139.8 123.2 %collective-permute-start.6 = (bf16[1,256,768]{2,1,0:T(8,128)(2,1)}, bf16[1,256,768]{2,1,0:T(8,128)(2,1)S(1)}, u32[]{:S(2)}, u32[]{:S(2)}) collective-permute-start(bf16[1,256,768]{2,1,0:T(8,128)(2,1)} %get-tuple-element.146), channel_id=1, source_target_pairs={{0,4},{4,8},{8,12},{12,16},{16,20},{20,24},{24,28},{28,0},{1,5},{5... | collective-permute-start | bytes 1179656 | tf_op jit(solution)/shard_map/ppermute | solution.py:22
  181.1 80.3 %collective-permute-start.4 = (bf16[1,256,768]{2,1,0:T(8,128)(2,1)}, bf16[1,256,768]{2,1,0:T(8,128)(2,1)S(1)}, u32[]{:S(2)}, u32[]{:S(2)}) collective-permute-start(bf16[1,256,768]{2,1,0:T(8,128)(2,1)} %get-tuple-element.148), channel_id=1, source_target_pairs={{0,12},{4,16},{8,20},{12,24},{16,28},{20,0},{24,4},{28,8},{1,13},{... | collective-permute-start | bytes 1179656 | tf_op jit(solution)/shard_map/ppermute | solution.py:22
  228.3 33.9 %collective-permute-start.5 = (bf16[1,256,768]{2,1,0:T(8,128)(2,1)}, bf16[1,256,768]{2,1,0:T(8,128)(2,1)S(1)}, u32[]{:S(2)}, u32[]{:S(2)}) collective-permute-start(bf16[1,256,768]{2,1,0:T(8,128)(2,1)} %get-tuple-element.147), channel_id=1, source_target_pairs={{0,8},{4,12},{8,16},{12,20},{16,24},{20,28},{24,0},{28,4},{1,9},{5... | collective-permute-start | bytes 1179656 | tf_op jit(solution)/shard_map/ppermute | solution.py:22
  265.6 75.2 %all-to-all-start.3 = ((bf16[128,4,768]{0,2,1:T(8,128)(2,1)}), bf16[128,4,768]{0,2,1:T(8,128)(2,1)S(1)}, u32[]{:S(2)}, u32[]{:S(2)}) async-start(bf16[128,4,768]{0,2,1:T(8,128)(2,1)} %bitcast.201), calls=%async_computation.3 | async-start | bytes 1572864 | tf_op jit(solution)/shard_map/all_to_all | solution.py:100
  340.8 57.6 %all-to-all-start.6 = ((bf16[128,4,768]{0,2,1:T(8,128)(2,1)}), bf16[128,4,768]{0,2,1:T(8,128)(2,1)S(1)}, u32[]{:S(2)}, u32[]{:S(2)}) async-start(bf16[128,4,768]{0,2,1:T(8,128)(2,1)} %bitcast.21), calls=%async_computation.6 | async-start | bytes 1572864 | tf_op jit(solution)/shard_map/all_to_all | solution.py:103
  398.4 28.7 %all-to-all-start.4 = ((bf16[4,128,768]{1,2,0:T(8,128)(2,1)}), bf16[4,128,768]{1,2,0:T(8,128)(2,1)S(1)}, u32[]{:S(2)}, u32[]{:S(2)}) async-start(bf16[4,128,768]{1,2,0:T(8,128)(2,1)} %bitcast.17), calls=%async_computation.4 | async-start | bytes 1572864 | tf_op jit(solution)/shard_map/all_to_all | solution.py:342
  427.1 100.3 %all-to-all-start.7 = ((bf16[4,128,768]{1,2,0:T(8,128)(2,1)}), bf16[4,128,768]{1,2,0:T(8,128)(2,1)S(1)}, u32[]{:S(2)}, u32[]{:S(2)}) async-start(bf16[4,128,768]{1,2,0:T(8,128)(2,1)} %bitcast.211), calls=%async_computation.7 | async-start | bytes 1572864 | tf_op jit(solution)/shard_map/all_to_all | solution.py:343
  528.3 143.7 %all-to-all-start.10 = ((f32[8,256,768]{2,1,0:T(8,128)}), f32[8,256,768]{2,1,0:T(8,128)}, u32[]{:S(2)}, u32[]{:S(2)}) async-start(f32[8,256,768]{2,1,0:T(8,128)} %bitcast.166), calls=%async_computation.10 | async-start | bytes 12582912 | tf_op jit(solution)/shard_map/all_to_all | solution.py:251
  672.1 255.4 %all-to-all-start.8 = ((f32[8,256,768]{2,1,0:T(8,128)}), f32[8,256,768]{2,1,0:T(8,128)}, u32[]{:S(2)}, u32[]{:S(2)}) async-start(f32[8,256,768]{2,1,0:T(8,128)} %bitcast.165), calls=%async_computation.8 | async-start | bytes 12582912 | tf_op jit(solution)/shard_map/all_to_all | solution.py:244
  677.1 207.6 %all-reduce.4.cloned.1.call-start = ((), (), s32[]{:S(2)}) async-start(), calls=%async_computation.12 | async-start | bytes 1572864 | tf_op jit(solution)/shard_map/psum | solution.py:294
  796.2 172.2 %all-reduce.6.cloned.1.call-start = ((), (), s32[]{:S(2)}) async-start(), calls=%async_computation.13 | async-start | bytes 4718592 | tf_op jit(solution)/shard_map/psum | solution.py:318
  927.5 56.0 %all-to-all-start.11 = ((bf16[4,128,768]{2,1,0:T(8,128)(2,1)}), bf16[4,128,768]{2,1,0:T(8,128)(2,1)}, u32[]{:S(2)}, u32[]{:S(2)}) async-start(bf16[4,128,768]{2,1,0:T(8,128)(2,1)} %convert_element_type.127), calls=%async_computation.11 | async-start | bytes 1572864 | tf_op jit(solution)/shard_map/all_to_all | solution.py:345
  983.5 13.3 %all-to-all-start.9 = ((bf16[4,128,768]{2,1,0:T(8,128)(2,1)}), bf16[4,128,768]{2,1,0:T(8,128)(2,1)S(1)}, u32[]{:S(2)}, u32[]{:S(2)}) async-start(bf16[4,128,768]{2,1,0:T(8,128)(2,1)} %convert_element_type.123), calls=%async_computation.9 | async-start | bytes 1572864 | tf_op jit(solution)/shard_map/all_to_all | solution.py:344
  (42 other events, 519.2 us)
Sparse Core Ops, SparseCore 0:
  796.3 88.3 all-reduce.3
  902.2 66.1 all-reduce.5
